TPU v7x, 32 devices: a whole 2x2x4 slice. The times are simulated.
32 devices in a mesh: dp: 4 (over y, core), ctx: 8 (over z, x).
Axes of the slice: x: 2, y: 2, z: 4, core: 2. Of those that a mesh axis runs over, the one named last changes fastest.
Arguments:
- layer_input: bfloat16 [8, 1024, 1024], P('dp', 'ctx'), may hold values from -6 to 6
- doc_ids: int32 [8, 1024], P('dp'), may hold values from 0 to 4, as said below
- attn_gain: bfloat16 [1024], P(('dp', 'ctx')), may hold values from 0.099609375 to 1.8984375
- query_weight: bfloat16 [1024, 1024], P(('dp', 'ctx')), may hold values from -0.25 to 0.25
- key_weight: bfloat16 [1024, 1024], P(('dp', 'ctx')), may hold values from -0.1875 to 0.1875
- value_weight: bfloat16 [1024, 1024], P(('dp', 'ctx')), may hold values from -0.1875 to 0.1875
- out_weight: bfloat16 [1024, 1024], P(('dp', 'ctx')), may hold values from -1.5 to 1.5
- mlp_gain: bfloat16 [1024], P(('dp', 'ctx')), may hold values from 0.099609375 to 1.8984375
- gate_weight: bfloat16 [1024, 4096], P(('dp', 'ctx')), may hold values from -0.1875 to 0.1875
- up_weight: bfloat16 [1024, 4096], P(('dp', 'ctx')), may hold values from -0.1875 to 0.1875
- down_weight: bfloat16 [4096, 1024], P(('dp', 'ctx')), may hold values from -0.1875 to 0.1875
- out_grad: bfloat16 [8, 1024, 1024], P('dp', 'ctx'), may hold values from -6 to 6
Outputs:
- layer_output: bfloat16 [8, 1024, 1024], P('dp', 'ctx')
- input_grad: float32 [8, 1024, 1024], P('dp', 'ctx')
- attn_gain_grad: float32 [1024], P(('dp', 'ctx'))
- query_grad: float32 [1024, 1024], P(('dp', 'ctx'))
- key_grad: float32 [1024, 1024], P(('dp', 'ctx'))
- value_grad: float32 [1024, 1024], P(('dp', 'ctx'))
- out_proj_grad: float32 [1024, 1024], P(('dp', 'ctx'))
- mlp_gain_grad: float32 [1024], P(('dp', 'ctx'))
- gate_grad: float32 [1024, 4096], P(('dp', 'ctx'))
- up_grad: float32 [1024, 4096], P(('dp', 'ctx'))
- down_grad: float32 [4096, 1024], P(('dp', 'ctx'))
Inputs may be any that keep to these rules, and one draw needn't show every extreme that they name: Within each sequence doc_ids start at 0 and never fall; the rows of one value form one document of 60 to 800 rows, except the document at one end of a sequence, which may be shorter; every sequence holds one document of exactly 800 rows, at its start or at its end; in the first sequence all other documents but the one at its other end have exactly 60 rows.
All inputs are finite; a program needn't handle non-finite values.
Results may differ from a plain program's by a relative error of at most 0.015.
Values may be sent and summed in bfloat16 or wider, within the bound.
A program may use at most 256 MiB of HBM per device.

v0:
```python
import jax
import jax.numpy as jnp
from jax import lax
from jax.sharding import PartitionSpec as P

HEAD = 64
EPS = 1e-05


def product(left, right):
    return jnp.dot(left, right, preferred_element_type=jnp.float32)


def product_left(left, right):
    return lax.dot_general(
        left, right, (((0,), (0,)), ((), ())), preferred_element_type=jnp.float32
    )


def product_right(left, right):
    return lax.dot_general(
        left, right, (((1,), (1,)), ((), ())), preferred_element_type=jnp.float32
    )


def normalize(rows, gain):
    inverse = lax.rsqrt(jnp.mean(rows * rows, axis=-1, keepdims=True) + EPS)
    return (rows * inverse * gain, inverse)


def norm_back(rows, inverse, gain, upstream):
    normed = rows * inverse
    scaled = upstream * gain
    grad_rows = inverse * (scaled - normed * jnp.mean(scaled * normed, axis=-1, keepdims=True))
    return (grad_rows, jnp.sum(upstream * normed, axis=0))


def head_pair(array, start):
    piece = lax.dynamic_slice_in_dim(array, start, 2 * HEAD, 2)
    return piece.reshape(array.shape[0], array.shape[1], 2, HEAD)


def pair_scores(query, keys, allowed, start):
    scores = jnp.einsum(
        "sqhd,skhd->shqk",
        head_pair(query, start),
        head_pair(keys, start),
        preferred_element_type=jnp.float32,
    ) * HEAD ** (-0.5)
    return jnp.where(allowed[:, None], scores, -1e30)


def attend(query, keys, values, allowed):
    groups, rows, width = query.shape

    def step(index, carry):
        mixed_all, logsum = carry
        start = index * 2 * HEAD
        scores = pair_scores(query, keys, allowed, start)
        top = jnp.max(scores, axis=-1, keepdims=True)
        lifted = jnp.exp(scores - top)
        total = jnp.sum(lifted, axis=-1, keepdims=True)
        probs = (lifted / total).astype(jnp.bfloat16)
        mixed = jnp.einsum(
            "shqk,skhd->sqhd", probs, head_pair(values, start), preferred_element_type=jnp.float32
        )
        mixed_all = lax.dynamic_update_slice_in_dim(
            mixed_all, mixed.reshape(groups, rows, 2 * HEAD).astype(jnp.bfloat16), start, 2
        )
        logsum = lax.dynamic_update_slice_in_dim(
            logsum, (top + jnp.log(total))[..., 0], index * 2, 1
        )
        return (mixed_all, logsum)

    start_state = (
        jnp.zeros((groups, rows, width), jnp.bfloat16),
        jnp.zeros((groups, width // HEAD, rows), jnp.float32),
    )
    return lax.fori_loop(0, width // (2 * HEAD), step, start_state)


def attend_back(query, keys, values, allowed, logsum, grad_mixed):
    groups, rows, width = query.shape
    length = keys.shape[1]
    scale = HEAD ** (-0.5)

    def step(index, carry):
        grad_query, grad_keys, grad_values = carry
        start = index * 2 * HEAD
        scores = pair_scores(query, keys, allowed, start)
        kept = lax.dynamic_slice_in_dim(logsum, index * 2, 2, 1)
        probs = jnp.exp(scores - kept[..., None])
        upstream = head_pair(grad_mixed, start)
        grad_probs = jnp.einsum(
            "sqhd,skhd->shqk",
            upstream,
            head_pair(values, start),
            preferred_element_type=jnp.float32,
        )
        grad_scores = (
            probs * (grad_probs - jnp.sum(probs * grad_probs, axis=-1, keepdims=True))
        ).astype(jnp.bfloat16)
        part_query = (
            jnp.einsum(
                "shqk,skhd->sqhd",
                grad_scores,
                head_pair(keys, start),
                preferred_element_type=jnp.float32,
            )
            * scale
        )
        part_keys = (
            jnp.einsum(
                "shqk,sqhd->skhd",
                grad_scores,
                head_pair(query, start),
                preferred_element_type=jnp.float32,
            )
            * scale
        )
        part_values = jnp.einsum(
            "shqk,sqhd->skhd",
            probs.astype(jnp.bfloat16),
            upstream,
            preferred_element_type=jnp.float32,
        )
        grad_query = lax.dynamic_update_slice_in_dim(
            grad_query, part_query.reshape(groups, rows, 2 * HEAD), start, 2
        )
        grad_keys = lax.dynamic_update_slice_in_dim(
            grad_keys, part_keys.reshape(groups, length, 2 * HEAD), start, 2
        )
        grad_values = lax.dynamic_update_slice_in_dim(
            grad_values, part_values.reshape(groups, length, 2 * HEAD), start, 2
        )
        return (grad_query, grad_keys, grad_values)

    start_state = (
        jnp.zeros((groups, rows, width), jnp.float32),
        jnp.zeros((groups, length, width), jnp.float32),
        jnp.zeros((groups, length, width), jnp.float32),
    )
    return lax.fori_loop(0, width // (2 * HEAD), step, start_state)


def on_device(
    layer_input,
    doc_ids,
    attn_gain,
    query_weight,
    key_weight,
    value_weight,
    out_weight,
    mlp_gain,
    gate_weight,
    up_weight,
    down_weight,
    out_grad,
):
    groups, rows, width = layer_input.shape
    length = doc_ids.shape[1]
    gathered = (
        lax.all_gather(attn_gain, ("dp", "ctx"), axis=0, tiled=True),
        lax.all_gather(query_weight, ("dp", "ctx"), axis=0, tiled=True),
        lax.all_gather(key_weight, ("dp", "ctx"), axis=0, tiled=True),
        lax.all_gather(value_weight, ("dp", "ctx"), axis=0, tiled=True),
        lax.all_gather(out_weight, ("dp", "ctx"), axis=0, tiled=True),
        lax.all_gather(mlp_gain, ("dp", "ctx"), axis=0, tiled=True),
        lax.all_gather(gate_weight, ("dp", "ctx"), axis=0, tiled=True),
        lax.all_gather(up_weight, ("dp", "ctx"), axis=0, tiled=True),
        lax.all_gather(down_weight, ("dp", "ctx"), axis=0, tiled=True),
    )
    gain_one, w_query, w_key, w_value, w_out, gain_two, w_gate, w_up, w_down = gathered
    first = lax.axis_index("ctx") * rows
    places = jnp.arange(length)
    own_ids = lax.dynamic_slice_in_dim(doc_ids, first, rows, 1)
    own_places = first + jnp.arange(rows)
    allowed = (own_ids[:, :, None] == doc_ids[:, None, :]) & (
        places[None, None, :] <= own_places[None, :, None]
    )
    inputs = layer_input.reshape(groups * rows, width).astype(jnp.float32)
    gain_attn = gain_one.astype(jnp.float32)
    normed_full, inverse_one = normalize(inputs, gain_attn)
    normed = normed_full.astype(jnp.bfloat16)
    query = product(normed, w_query).astype(jnp.bfloat16).reshape(groups, rows, width)
    keys_own = product(normed, w_key).astype(jnp.bfloat16).reshape(groups, rows, width)
    values_own = product(normed, w_value).astype(jnp.bfloat16).reshape(groups, rows, width)
    keys, values = (
        lax.all_gather(keys_own, "ctx", axis=1, tiled=True),
        lax.all_gather(values_own, "ctx", axis=1, tiled=True),
    )
    attended, logsum = attend(query, keys, values, allowed)
    attended_rows = attended.reshape(groups * rows, width)
    middle = inputs + product(attended_rows, w_out)
    gain_mlp = gain_two.astype(jnp.float32)
    normed_two_full, inverse_two = normalize(middle, gain_mlp)
    normed_two = normed_two_full.astype(jnp.bfloat16)
    gate = product(normed_two, w_gate)
    upward = product(normed_two, w_up)
    sigma = jax.nn.sigmoid(gate)
    hidden = (gate * sigma * upward).astype(jnp.bfloat16)
    layer_output = (middle + product(hidden, w_down)).astype(jnp.bfloat16)
    gathered_back = (
        lax.all_gather(attn_gain, ("dp", "ctx"), axis=0, tiled=True),
        lax.all_gather(query_weight, ("dp", "ctx"), axis=0, tiled=True),
        lax.all_gather(key_weight, ("dp", "ctx"), axis=0, tiled=True),
        lax.all_gather(value_weight, ("dp", "ctx"), axis=0, tiled=True),
        lax.all_gather(out_weight, ("dp", "ctx"), axis=0, tiled=True),
        lax.all_gather(mlp_gain, ("dp", "ctx"), axis=0, tiled=True),
        lax.all_gather(gate_weight, ("dp", "ctx"), axis=0, tiled=True),
        lax.all_gather(up_weight, ("dp", "ctx"), axis=0, tiled=True),
        lax.all_gather(down_weight, ("dp", "ctx"), axis=0, tiled=True),
    )
    gain_one, w_query, w_key, w_value, w_out, gain_two, w_gate, w_up, w_down = gathered_back
    upstream = out_grad.reshape(groups * rows, width)
    down_grad = product_left(hidden, upstream)
    grad_hidden = product_right(upstream, w_down)
    grad_gate = (grad_hidden * upward * sigma * (1.0 + gate * (1.0 - sigma))).astype(jnp.bfloat16)
    grad_up = (grad_hidden * gate * sigma).astype(jnp.bfloat16)
    gate_grad = product_left(normed_two, grad_gate)
    up_grad = product_left(normed_two, grad_up)
    grad_normed_two = product_right(grad_gate, w_gate) + product_right(grad_up, w_up)
    grad_middle, mlp_gain_grad = norm_back(
        middle, inverse_two, gain_two.astype(jnp.float32), grad_normed_two
    )
    grad_middle = grad_middle + upstream.astype(jnp.float32)
    grad_branch = grad_middle.astype(jnp.bfloat16)
    out_proj_grad = product_left(attended_rows, grad_branch)
    grad_attended = (
        product_right(grad_branch, w_out).astype(jnp.bfloat16).reshape(groups, rows, width)
    )
    grad_query, grad_keys_all, grad_values_all = attend_back(
        query, keys, values, allowed, logsum, grad_attended
    )
    grad_keys, grad_values = (
        lax.psum_scatter(
            grad_keys_all.astype(jnp.bfloat16), "ctx", scatter_dimension=1, tiled=True
        ).astype(jnp.float32),
        lax.psum_scatter(
            grad_values_all.astype(jnp.bfloat16), "ctx", scatter_dimension=1, tiled=True
        ).astype(jnp.float32),
    )
    grad_query = grad_query.astype(jnp.bfloat16).reshape(groups * rows, width)
    grad_keys = grad_keys.astype(jnp.bfloat16).reshape(groups * rows, width)
    grad_values = grad_values.astype(jnp.bfloat16).reshape(groups * rows, width)
    query_grad = product_left(normed, grad_query)
    key_grad = product_left(normed, grad_keys)
    value_grad = product_left(normed, grad_values)
    grad_normed = (
        product_right(grad_query, w_query)
        + product_right(grad_keys, w_key)
        + product_right(grad_values, w_value)
    )
    grad_inputs, attn_gain_grad = norm_back(
        inputs, inverse_one, gain_one.astype(jnp.float32), grad_normed
    )
    input_grad = (grad_middle + grad_inputs).reshape(groups, rows, width)
    shares = (
        lax.psum_scatter(attn_gain_grad, ("dp", "ctx"), scatter_dimension=0, tiled=True),
        lax.psum_scatter(query_grad, ("dp", "ctx"), scatter_dimension=0, tiled=True),
        lax.psum_scatter(key_grad, ("dp", "ctx"), scatter_dimension=0, tiled=True),
        lax.psum_scatter(value_grad, ("dp", "ctx"), scatter_dimension=0, tiled=True),
        lax.psum_scatter(out_proj_grad, ("dp", "ctx"), scatter_dimension=0, tiled=True),
        lax.psum_scatter(mlp_gain_grad, ("dp", "ctx"), scatter_dimension=0, tiled=True),
        lax.psum_scatter(gate_grad, ("dp", "ctx"), scatter_dimension=0, tiled=True),
        lax.psum_scatter(up_grad, ("dp", "ctx"), scatter_dimension=0, tiled=True),
        lax.psum_scatter(down_grad, ("dp", "ctx"), scatter_dimension=0, tiled=True),
    )
    return (
        layer_output.reshape(groups, rows, width),
        input_grad,
        shares[0],
        shares[1],
        shares[2],
        shares[3],
        shares[4],
        shares[5],
        shares[6],
        shares[7],
        shares[8],
    )


def solution(mesh):
    placed = (
        P("dp", "ctx", None),
        P("dp", None),
        P(("dp", "ctx")),
        P(("dp", "ctx"), None),
        P(("dp", "ctx"), None),
        P(("dp", "ctx"), None),
        P(("dp", "ctx"), None),
        P(("dp", "ctx")),
        P(("dp", "ctx"), None),
        P(("dp", "ctx"), None),
        P(("dp", "ctx"), None),
        P("dp", "ctx", None),
    )
    return jax.shard_map(
        on_device,
        mesh=mesh,
        in_specs=placed,
        out_specs=(
            P("dp", "ctx", None),
            P("dp", "ctx", None),
            P(("dp", "ctx")),
            P(("dp", "ctx"), None),
            P(("dp", "ctx"), None),
            P(("dp", "ctx"), None),
            P(("dp", "ctx"), None),
            P(("dp", "ctx")),
            P(("dp", "ctx"), None),
            P(("dp", "ctx"), None),
            P(("dp", "ctx"), None),
        ),
        check_vma=False,
    )
```

profile of v0, /device:TPU:0, one launch (start us, length us, event | category | flops | bytes accessed | tf_op | source)
XLA Modules:
  0.0 2608.5 jit_solution(7120969927249212955)
XLA Ops:
  11.1 42.1 %all-reduce.5 = (bf16[1024]{0:T(1024)(128)(2,1)S(1)}, bf16[1024]{0:T(1024)(128)(2,1)S(1)}) all-reduce(bf16[1024]{0:T(1024)(128)(2,1)S(1)} %dynamic-update-slice, bf16[1024]{0:T(1024)(128)(2,1)S(1)} %dynamic-update-slice.1), channel_id=1, replica_groups=mesh['dp'=4,'ctx'=8] {'dp','ctx'}, use_global_device_ids=true, to_apply=%add | all-reduce | flops 2048 | bytes 8192
  55.8 14.4 all-gather.10.cloned.1.call-done
  70.3 2.3 convolution_convert_fusion.4
  73.7 55.0 %all-gather.16.cloned.1.call-done = bf16[1024,1024]{1,0:T(8,128)(2,1)} async-done(((bf16[32,1024]{1,0:T(8,128)(2,1)}), bf16[1024,1024]{1,0:T(8,128)(2,1)}) %all-gather.16.cloned.1.call-update) | async-done | bytes 2097168 | tf_op jit(solution)/shard_map/all_gather | solution.py:165
  128.7 2.3 convolution_convert_fusion.2
  135.4 51.7 %all-gather.14.cloned.1.call-done = bf16[1024,1024]{1,0:T(8,128)(2,1)} async-done(((bf16[32,1024]{1,0:T(8,128)(2,1)}), bf16[1024,1024]{1,0:T(8,128)(2,1)}) %all-gather.14.cloned.1.call-update) | async-done | bytes 2097168 | tf_op jit(solution)/shard_map/all_gather | solution.py:164
  187.1 2.3 convolution_convert_fusion.3
  190.4 73.1 %all-gather.12.cloned.1.call-done = bf16[2,1024,1024]{1,2,0:T(8,128)(2,1)} async-done(((bf16[2,128,1024]{1,2,0:T(8,128)(2,1)}), bf16[2,1024,1024]{1,2,0:T(8,128)(2,1)}) %all-gather.12.cloned.1.call-update) | async-done | bytes 4194320 | tf_op jit(solution)/shard_map/all_gather | solution.py:190
  263.4 75.7 %all-gather.18.cloned.1.call-done = bf16[2,1024,1024]{1,2,0:T(8,128)(2,1)} async-done(((bf16[2,128,1024]{1,2,0:T(8,128)(2,1)}), bf16[2,1024,1024]{1,2,0:T(8,128)(2,1)}) %all-gather.18.cloned.1.call-update) | async-done | bytes 4194320 | tf_op jit(solution)/shard_map/all_gather | solution.py:189
  340.0 56.5 %while.38 = (s32[]{:T(128)}, bf16[2,128,1024]{2,1,0:T(8,128)(2,1)}, f32[2,16,128]{2,1,0:T(8,128)S(1)}, bf16[2,1024,1024]{1,2,0:T(8,128)(2,1)}, bf16[2,128,1024]{...) while((s32[]{:T(128)}, bf16[2,128,1024]{2,1,0:T(8,128)(2,1)}, ...), condition=%wide.region_4.5_spmd.clone, body=%wide.region_1.4_spmd.clone.sunk | while | flops 141065728 | bytes 11166969 | solution.py:79
  340.0 2.2 constant_dynamic-slice_fusion.16
  347.1 2.1 constant_dynamic-slice_fusion.16
  354.2 2.1 constant_dynamic-slice_fusion.16
  368.3 2.1 constant_dynamic-slice_fusion.16
  375.3 2.1 constant_dynamic-slice_fusion.16
  382.4 2.1 constant_dynamic-slice_fusion.16
  389.4 2.1 constant_dynamic-slice_fusion.16
  396.9 2.6 multiply_reduce_fusion.5
  399.7 76.4 %all-gather.22.cloned.1.call-done = bf16[1024,4096]{1,0:T(8,128)(2,1)} async-done(((bf16[32,4096]{1,0:T(8,128)(2,1)}), bf16[1024,4096]{1,0:T(8,128)(2,1)}) %all-gather.22.cloned.1.call-update) | async-done | bytes 8388624 | tf_op jit(solution)/shard_map/all_gather | solution.py:169
  476.1 7.7 fusion.17
  483.8 71.3 %all-gather.24.cloned.1.call-done = bf16[1024,4096]{1,0:T(8,128)(2,1)} async-done(((bf16[32,4096]{1,0:T(8,128)(2,1)}), bf16[1024,4096]{1,0:T(8,128)(2,1)}) %all-gather.24.cloned.1.call-update) | async-done | bytes 8388624 | tf_op jit(solution)/shard_map/all_gather | solution.py:170
  555.1 7.7 fusion.18
  562.8 71.3 %all-gather.26.cloned.1.call-done = bf16[4096,1024]{1,0:T(8,128)(2,1)} async-done(((bf16[128,1024]{1,0:T(8,128)(2,1)}), bf16[4096,1024]{1,0:T(8,128)(2,1)}) %all-gather.26.cloned.1.call-update) | async-done | bytes 8388624 | tf_op jit(solution)/shard_map/all_gather | solution.py:171
  634.1 12.9 multiply_convert_fusion.1
  647.0 7.3 fusion.19
  654.3 2.6 multiply_reduce_fusion.1
  660.5 2.5 broadcast.154.clone
  663.0 2.6 broadcast.154.clone2
  666.4 99.2 %while.39 = (s32[]{:T(128)}, bf16[2,128,1024]{2,1,0:T(8,128)(2,1)}, bf16[2,1024,1024]{2,1,0:T(8,128)(2,1)}, bf16[2,1024,1024]{2,1,0:T(8,128)(2,1)}, bf16[2,1024,...) while((s32[]{:T(128)}, bf16[2,128,1024]{2,1,0:T(8,128)(2,1)}, ...), condition=%wide.region_9.0_spmd.clone, body=%wide.region_7.0_spmd.clone.sunk | while | flops 341376512 | bytes 38882672 | solution.py:143
  766.8 2.8 convolution_bitcast_fusion.2
  771.0 2.7 fusion.12
  773.9 78.4 %reduce-scatter.10.cloned.1.call-done = bf16[2,128,1024]{2,1,0:T(8,128)(2,1)} async-done(((bf16[2,1024,1024]{2,1,0:T(8,128)(2,1)}), bf16[2,128,1024]{2,1,0:T(8,128)(2,1)}) %reduce-scatter.10.cloned.1.call-update) | async-done | bytes 524304 | tf_op jit(solution)/shard_map/reduce_scatter | solution.py:236
  852.4 3.8 convolution_bitcast_fusion.1
  856.3 88.0 %reduce-scatter.12.cloned.1.call-done = bf16[2,128,1024]{2,1,0:T(8,128)(2,1)} async-done(((bf16[2,1024,1024]{2,1,0:T(8,128)(2,1)}), bf16[2,128,1024]{2,1,0:T(8,128)(2,1)}) %reduce-scatter.12.cloned.1.call-update) | async-done | bytes 524304 | tf_op jit(solution)/shard_map/reduce_scatter | solution.py:239
  944.3 3.9 convolution_bitcast_fusion
  949.2 9.7 fusion.21
  959.0 9.7 fusion.22
  969.8 9.7 fusion.23
  979.5 2.5 fusion.20
  982.1 6.7 fusion.11
  991.7 42.6 %all-reduce.4 = (f32[1024]{0:T(1024)S(1)}, f32[1024]{0:T(1024)S(1)}) all-reduce(f32[1024]{0:T(1024)S(1)} %get-tuple-element.554, f32[1024]{0:T(1024)S(1)} %get-tuple-element.552), channel_id=4, replica_groups=mesh['dp'=4,'ctx'=8] {'dp','ctx'}, use_global_device_ids=true, to_apply=%region_14.15.clone | all-reduce | flops 2048 | bytes 16384
  1036.6 54.6 %reduce-scatter.14.cloned.1.call-done = f32[32,1024]{1,0:T(8,128)} async-done(((f32[1024,1024]{1,0:T(8,128)}), f32[32,1024]{1,0:T(8,128)}) %reduce-scatter.14.cloned.1.call-update) | async-done | bytes 131088 | tf_op jit(solution)/shard_map/reduce_scatter | solution.py:260
  1091.3 143.7 %reduce-scatter.20.cloned.1.call-done = f32[32,1024]{1,0:T(8,128)} async-done(((f32[1024,1024]{1,0:T(8,128)}), f32[32,1024]{1,0:T(8,128)}) %reduce-scatter.20.cloned.1.call-update) | async-done | bytes 131088 | tf_op jit(solution)/shard_map/reduce_scatter | solution.py:263
  1234.9 143.8 %reduce-scatter.16.cloned.1.call-done = f32[32,1024]{1,0:T(8,128)} async-done(((f32[1024,1024]{1,0:T(8,128)}), f32[32,1024]{1,0:T(8,128)}) %reduce-scatter.16.cloned.1.call-update) | async-done | bytes 131088 | tf_op jit(solution)/shard_map/reduce_scatter | solution.py:261
  1378.7 143.8 %reduce-scatter.18.cloned.1.call-done = f32[32,1024]{1,0:T(8,128)} async-done(((f32[1024,1024]{1,0:T(8,128)}), f32[32,1024]{1,0:T(8,128)}) %reduce-scatter.18.cloned.1.call-update) | async-done | bytes 131088 | tf_op jit(solution)/shard_map/reduce_scatter | solution.py:262
  1522.6 358.7 %reduce-scatter.22.cloned.1.call-done = f32[32,4096]{1,0:T(8,128)} async-done(((f32[1024,4096]{1,0:T(8,128)}), f32[32,4096]{1,0:T(8,128)}) %reduce-scatter.22.cloned.1.call-update) | async-done | bytes 524304 | tf_op jit(solution)/shard_map/reduce_scatter | solution.py:265
  1881.3 360.0 %reduce-scatter.24.cloned.1.call-done = f32[32,4096]{1,0:T(8,128)} async-done(((f32[1024,4096]{1,0:T(8,128)}), f32[32,4096]{1,0:T(8,128)}) %reduce-scatter.24.cloned.1.call-update) | async-done | bytes 524304 | tf_op jit(solution)/shard_map/reduce_scatter | solution.py:266
  2241.3 360.1 %reduce-scatter.26.cloned.1.call-done = f32[128,1024]{1,0:T(8,128)} async-done(((f32[4096,1024]{1,0:T(8,128)}), f32[128,1024]{1,0:T(8,128)}) %reduce-scatter.26.cloned.1.call-update) | async-done | bytes 524304 | tf_op jit(solution)/shard_map/reduce_scatter | solution.py:267
  (371 shorter events, 168.6 us)
Async XLA Ops:
  7.2 63.1 %all-gather.10.cloned.1.call-start = ((), (), s32[]{:S(2)}) async-start(), calls=%async_computation.9 | async-start | bytes 2162688 | tf_op jit(solution)/shard_map/all_gather | solution.py:166
  7.9 120.8 %all-gather.16.cloned.1.call-start = ((), (), s32[]{:S(2)}) async-start(), calls=%async_computation.12 | async-start | bytes 2162688 | tf_op jit(solution)/shard_map/all_gather | solution.py:165
  8.7 178.4 %all-gather.14.cloned.1.call-start = ((), (), s32[]{:S(2)}) async-start(), calls=%async_computation.11 | async-start | bytes 2162688 | tf_op jit(solution)/shard_map/all_gather | solution.py:164
  9.4 254.1 %all-gather.12.cloned.1.call-start = ((), (), s32[]{:S(2)}) async-start(), calls=%async_computation.10 | async-start | bytes 4718592 | tf_op jit(solution)/shard_map/all_gather | solution.py:190
  54.5 18.2 copy-start.24
  73.6 265.5 %all-gather.18.cloned.1.call-start = ((), (), s32[]{:S(2)}) async-start(), calls=%async_computation.13 | async-start | bytes 4718592 | tf_op jit(solution)/shard_map/all_gather | solution.py:189
  131.0 4.4 copy-start.23
  132.0 264.8 %all-gather.20.cloned.1.call-start = ((), (), s32[]{:S(2)}) async-start(), calls=%async_computation.14 | async-start | bytes 2162688 | tf_op jit(solution)/shard_map/all_gather | solution.py:167
  132.6 343.4 %all-gather.22.cloned.1.call-start = ((), (), s32[]{:S(2)}) async-start(), calls=%async_computation.15 | async-start | bytes 8650752 | tf_op jit(solution)/shard_map/all_gather | solution.py:169
  133.4 421.7 %all-gather.24.cloned.1.call-start = ((), (), s32[]{:S(2)}) async-start(), calls=%async_computation.16 | async-start | bytes 8650752 | tf_op jit(solution)/shard_map/all_gather | solution.py:170
  134.1 500.0 %all-gather.26.cloned.1.call-start = ((), (), s32[]{:S(2)}) async-start(), calls=%async_computation.17 | async-start | bytes 8650752 | tf_op jit(solution)/shard_map/all_gather | solution.py:171
  134.9 717.5 %reduce-scatter.10.cloned.1.call-start = ((), (), s32[]{:S(2)}) async-start(), calls=%async_computation.18 | async-start | bytes 4718592 | tf_op jit(solution)/shard_map/reduce_scatter | solution.py:236
  340.0 56.9 %copy-start.3 = (bf16[2,128,1024]{2,1,0:T(8,128)(2,1)S(1)}, bf16[2,128,1024]{2,1,0:T(8,128)(2,1)}, u32[]{:S(2)}) copy-start(bf16[2,128,1024]{2,1,0:T(8,128)(2,1)} %param.16) | copy-start | bytes 1572868
  399.5 257.5 %copy-start.7 = (f32[256,1024]{1,0:T(8,128)}, f32[256,1024]{1,0:T(8,128)S(1)}, u32[]{:S(2)}) copy-start(f32[256,1024]{1,0:T(8,128)S(1)} %get-tuple-element.616) | copy-start | bytes 3145732
  399.6 155.4 %copy-start.10 = (bf16[256,1024]{1,0:T(8,128)(2,1)}, bf16[256,1024]{1,0:T(8,128)(2,1)S(1)}, u32[]{:S(2)}) copy-start(bf16[256,1024]{1,0:T(8,128)(2,1)S(1)} %multiply_convert_fusion.5) | copy-start | bytes 1572868
  483.8 150.3 %copy-start.19 = (bf16[2,128,1024]{2,1,0:T(8,128)(2,1)S(1)}, bf16[2,128,1024]{2,1,0:T(8,128)(2,1)}, u32[]{:S(2)}) copy-start(bf16[2,128,1024]{2,1,0:T(8,128)(2,1)} %param.27) | copy-start | bytes 1572868
  647.0 7.3 copy-start.22
  647.0 7.3 copy-start.21
  647.0 7.3 copy-start.26
  657.0 2.0 copy-start.9
  670.0 2.2 copy-start.1
  676.1 1.4 copy-start.2
  682.4 2.2 copy-start.1
  688.5 1.5 copy-start.2
  694.8 2.2 copy-start.1
  700.9 1.5 copy-start.2
  707.3 2.2 copy-start.1
  719.7 2.2 copy-start.1
  732.0 2.2 copy-start.1
  738.1 1.4 copy-start.2
  744.4 2.2 copy-start.1
  750.5 1.4 copy-start.2
  756.8 2.2 copy-start.1
  762.9 1.4 copy-start.2
  765.6 178.7 %reduce-scatter.12.cloned.1.call-start = ((), (), s32[]{:S(2)}) async-start(), calls=%async_computation.19 | async-start | bytes 4718592 | tf_op jit(solution)/shard_map/reduce_scatter | solution.py:239
  766.3 325.0 %reduce-scatter.14.cloned.1.call-start = ((), (), s32[]{:S(2)}) async-start(), calls=%async_computation.20 | async-start | bytes 4325376 | tf_op jit(solution)/shard_map/reduce_scatter | solution.py:260
  769.6 465.3 %reduce-scatter.20.cloned.1.call-start = ((), (), s32[]{:S(2)}) async-start(), calls=%async_computation.23 | async-start | bytes 4325376 | tf_op jit(solution)/shard_map/reduce_scatter | solution.py:263
  773.7 605.0 %reduce-scatter.16.cloned.1.call-start = ((), (), s32[]{:S(2)}) async-start(), calls=%async_computation.21 | async-start | bytes 4325376 | tf_op jit(solution)/shard_map/reduce_scatter | solution.py:261
  856.3 666.3 %reduce-scatter.18.cloned.1.call-start = ((), (), s32[]{:S(2)}) async-start(), calls=%async_computation.22 | async-start | bytes 4325376 | tf_op jit(solution)/shard_map/reduce_scatter | solution.py:262
  948.2 933.1 %reduce-scatter.22.cloned.1.call-start = ((), (), s32[]{:S(2)}) async-start(), calls=%async_computation.24 | async-start | bytes 17301504 | tf_op jit(solution)/shard_map/reduce_scatter | solution.py:265
  959.0 1282.4 %reduce-scatter.24.cloned.1.call-start = ((), (), s32[]{:S(2)}) async-start(), calls=%async_computation.25 | async-start | bytes 17301504 | tf_op jit(solution)/shard_map/reduce_scatter | solution.py:266
  968.8 1632.7 %reduce-scatter.26.cloned.1.call-start = ((), (), s32[]{:S(2)}) async-start(), calls=%async_computation.26 | async-start | bytes 17301504 | tf_op jit(solution)/shard_map/reduce_scatter | solution.py:267
  979.5 2.5 copy-start.8
  979.5 2.6 copy-start.14
  982.1 6.7 copy-start.15
  982.1 6.7 copy-start.18
  988.8 1.8 copy-start.17
  988.8 1.8 copy-start.25
  (18 other events, 22.6 us)
Sparse Core Ops, SparseCore 0:
  11.0 59.2 all-gather.9
  73.3 55.3 all-gather.15
  131.7 55.3 all-gather.13
  189.5 73.8 all-gather.11
  265.9 73.1 all-gather.17
  342.0 54.8 all-gather.19
  399.9 76.1 all-gather.21
  479.0 75.9 all-gather.23
  558.1 75.9 all-gather.25
  765.7 86.6 reduce-scatter.9
  856.4 87.8 reduce-scatter.11
  947.0 144.2 reduce-scatter.13
  1094.1 140.7 reduce-scatter.19
  1237.6 141.0 reduce-scatter.15
  1381.4 141.1 reduce-scatter.17
  1525.3 355.9 reduce-scatter.21
  1884.0 357.2 reduce-scatter.23
  2244.0 357.3 reduce-scatter.25
where the time goes:
time: 2620 us; the launch traced here: 2610 us
  waiting for transfers between devices  2230 us (85%)
  matrix products  155 us (6%)
  local copies, waits for them, and re-layouts  108 us (4%)
  blocking collectives  84.6 us (3%)
    reduce_scatter x1, waiting for transfers between devices, on_device(): lax.psum_scatter(down_grad, ('dp', 'ctx'), scatter_dimension=0, tiled=True)  360 us
    reduce_scatter x1, waiting for transfers between devices, on_device(): lax.psum_scatter(up_grad, ('dp', 'ctx'), scatter_dimension=0, tiled=True)  360 us
    reduce_scatter x1, waiting for transfers between devices, on_device(): lax.psum_scatter(gate_grad, ('dp', 'ctx'), scatter_dimension=0, tiled=True)  359 us
    reduce_scatter x1, waiting for transfers between devices, on_device(): lax.psum_scatter(value_grad, ('dp', 'ctx'), scatter_dimension=0, tiled=True)  144 us
    reduce_scatter x1, waiting for transfers between devices, on_device(): lax.psum_scatter(key_grad, ('dp', 'ctx'), scatter_dimension=0, tiled=True)  144 us
    reduce_scatter x1, waiting for transfers between devices, on_device(): lax.psum_scatter(out_proj_grad, ('dp', 'ctx'), scatter_dimension=0, tiled...  144 us
    reduce_scatter x1, waiting for transfers between devices, on_device(): lax.psum_scatter(grad_values_all.astype(jnp.bfloat16), 'ctx', scatter_dim...  88 us
    unnamed x2, blocking collectives  84.6 us
  transfers between devices with their start and end apart: 18, of which 18 were waited for; matrix products, arithmetic and copies ran while one was open for 6% of the time, Pallas kernels for 0%

commit v1 on v0

--- a/solution.py
+++ b/solution.py
@@ -5,6 +5,34 @@
 
 HEAD = 64
 EPS = 1e-05
+
+
+def return_all_shapes(xs, dim_at):
+    xs = jnp.moveaxis(xs, 0, dim_at)
+    block_out = xs.shape
+    return xs.reshape(
+        *block_out[:dim_at], block_out[dim_at] * block_out[dim_at + 1], *block_out[dim_at + 2 :]
+    )
+
+
+def update_chunk(my_tile, lane_axis, join_dim):
+    extent = jax.lax.axis_size(lane_axis)
+    inbox = [(at, (at + 1) % extent) for at in range(extent)]
+    local_next, far_arr = ([], [])
+    so_far_all = [(ix, jj) for jj, ix in inbox]
+    for src_i in [*range(extent - 1)]:
+        if src_i % 2 == 0:
+            local_next.append(
+                jax.lax.ppermute(local_next[-1] if local_next else my_tile, lane_axis, inbox)
+            )
+        else:
+            far_arr.append(
+                jax.lax.ppermute(far_arr[-1] if far_arr else my_tile, lane_axis, perm=so_far_all)
+            )
+    mid_arr = jnp.stack([*local_next[::-1], my_tile, *far_arr], axis=0)
+    r1 = jax.lax.axis_index(lane_axis) - len(local_next)
+    mid_arr = mid_arr[(jnp.arange(extent) - r1) % extent]
+    return return_all_shapes(mid_arr, join_dim)
 
 
 def product(left, right):
@@ -187,7 +215,7 @@
     values_own = product(normed, w_value).astype(jnp.bfloat16).reshape(groups, rows, width)
     keys, values = (
         lax.all_gather(keys_own, "ctx", axis=1, tiled=True),
-        lax.all_gather(values_own, "ctx", axis=1, tiled=True),
+        update_chunk(values_own, "ctx", 1),
     )
     attended, logsum = attend(query, keys, values, allowed)
     attended_rows = attended.reshape(groups * rows, width)

time: 2620 us -> 2570 us (0.981)
  waiting for transfers between devices: 2230 us -> 2140 us
  starting transfers between devices: 1.4 us -> 28.7 us
    all_gather x1 -> x0, waiting for transfers between devices: 73.1 us -> none  [on_device(): lax.all_gather(values_own, 'ctx', axis=1, tiled=True)]
    ppermute x0 -> x7, waiting for transfers between devices: none -> 60.7 us  [the longest x4 52 us: update_chunk(): jax.lax.ppermute(local_next[-1] if local_next else my_tile, lane_axis, in...]
    all_gather x1, waiting for transfers between devices: 51.7 us -> 0.02 us  [on_device(): lax.all_gather(query_weight, ('dp', 'ctx'), axis=0, tiled=True)]
    all_gather x1, waiting for transfers between devices: 55 us -> 14 us  [on_device(): lax.all_gather(key_weight, ('dp', 'ctx'), axis=0, tiled=True)]
    all_gather x1, waiting for transfers between devices: 14.4 us -> 53.1 us  [on_device(): lax.all_gather(value_weight, ('dp', 'ctx'), axis=0, tiled=True)]
    all_gather x1, waiting for transfers between devices: 75.7 us -> 37.9 us  [on_device(): lax.all_gather(keys_own, 'ctx', axis=1, tiled=True)]
    ppermute x0 -> x7, starting transfers between devices: none -> 27.7 us  [the longest x3 21.2 us: update_chunk(): jax.lax.ppermute(far_arr[-1] if far_arr else my_tile, lane_axis, perm=so_...]
  transfers between devices with their start and end apart: 18 -> 24, of which waited for: 18 -> 21; matrix products, arithmetic and copies ran while one was open for 6% -> 6% of each run, Pallas kernels for 0% -> 0%
where the time goes in v1:
time: 2570 us; the launch traced here: 2560 us
  waiting for transfers between devices  2140 us (83%)
  matrix products  149 us (6%)
  local copies, waits for them, and re-layouts  122 us (5%)
  blocking collectives  84.3 us (3%)
  starting transfers between devices  28.7 us (1%)
    reduce_scatter x1, waiting for transfers between devices, on_device(): lax.psum_scatter(down_grad, ('dp', 'ctx'), scatter_dimension=0, tiled=True)  360 us
    reduce_scatter x1, waiting for transfers between devices, on_device(): lax.psum_scatter(up_grad, ('dp', 'ctx'), scatter_dimension=0, tiled=True)  360 us
    reduce_scatter x1, waiting for transfers between devices, on_device(): lax.psum_scatter(gate_grad, ('dp', 'ctx'), scatter_dimension=0, tiled=True)  359 us
    reduce_scatter x1, waiting for transfers between devices, on_device(): lax.psum_scatter(key_grad, ('dp', 'ctx'), scatter_dimension=0, tiled=True)  144 us
    reduce_scatter x1, waiting for transfers between devices, on_device(): lax.psum_scatter(value_grad, ('dp', 'ctx'), scatter_dimension=0, tiled=True)  144 us
    reduce_scatter x1, waiting for transfers between devices, on_device(): lax.psum_scatter(out_proj_grad, ('dp', 'ctx'), scatter_dimension=0, tiled...  143 us
    reduce_scatter x1, waiting for transfers between devices, on_device(): lax.psum_scatter(grad_values_all.astype(jnp.bfloat16), 'ctx', scatter_dim...  87.7 us
    unnamed x2, blocking collectives  84.3 us
  transfers between devices with their start and end apart: 24, of which 21 were waited for; matrix products, arithmetic and copies ran while one was open for 6% of the time, Pallas kernels for 0%

profile of v1, /device:TPU:0, one launch (start us, length us, event | category | flops | bytes accessed | tf_op | source)
XLA Modules:
  0.0 2558.3 jit_solution(722697486270216222)
XLA Ops:
  11.1 42.1 %all-reduce.5 = (bf16[1024]{0:T(1024)(128)(2,1)S(1)}, bf16[1024]{0:T(1024)(128)(2,1)S(1)}) all-reduce(bf16[1024]{0:T(1024)(128)(2,1)S(1)} %dynamic-update-slice, bf16[1024]{0:T(1024)(128)(2,1)S(1)} %dynamic-update-slice.1), channel_id=1, replica_groups=mesh['dp'=4,'ctx'=8] {'dp','ctx'}, use_global_device_ids=true, to_apply=%add | all-reduce | flops 2048 | bytes 8192
  56.3 14.0 all-gather.13.cloned.1.call-done
  75.6 53.1 %all-gather.9.cloned.1.call-done = bf16[1024,1024]{1,0:T(8,128)(2,1)} async-done(((bf16[32,1024]{1,0:T(8,128)(2,1)}), bf16[1024,1024]{1,0:T(8,128)(2,1)}) %all-gather.9.cloned.1.call-update) | async-done | bytes 2097168 | tf_op jit(solution)/shard_map/all_gather | solution.py:194
  132.5 16.1 collective-permute-done
  148.6 4.7 collective-permute-start.4
  153.3 19.2 collective-permute-done.1
  172.5 2.5 collective-permute-start.2
  175.2 11.6 collective-permute-start.5
  186.7 13.9 collective-permute-done.2
  203.3 3.1 convolution_convert_fusion.3
  208.4 4.9 collective-permute-start.6
  213.3 2.8 collective-permute-done.3
  224.1 8.8 collective-permute-done.6
  233.8 5.0 gather_fusion
  238.7 6.8 copy.46
  245.5 7.4 reshape.326
  252.9 37.9 %all-gather.15.cloned.1.call-done = bf16[2,1024,1024]{1,2,0:T(8,128)(2,1)} async-done(((bf16[2,128,1024]{1,2,0:T(8,128)(2,1)}), bf16[2,1024,1024]{1,2,0:T(8,128)(2,1)}) %all-gather.15.cloned.1.call-update) | async-done | bytes 4194320 | tf_op jit(solution)/shard_map/all_gather | solution.py:217
  290.9 37.4 %while.38 = (s32[]{:T(128)}, bf16[2,128,1024]{2,1,0:T(8,128)(2,1)S(1)}, f32[2,16,128]{2,1,0:T(8,128)S(1)}, bf16[2,1024,1024]{1,2,0:T(8,128)(2,1)}, bf16[2,128,10...) while((s32[]{:T(128)}, ...), condition=%wide.region_4.5_spmd.clone, body=%wide.region_1.4_spmd.clone.sunk | while | flops 141065728 | bytes 11166977 | solution.py:107
  328.4 20.0 all-gather.17.cloned.1.call-done
  351.0 76.5 %all-gather.19.cloned.1.call-done = bf16[1024,4096]{1,0:T(8,128)(2,1)} async-done(((bf16[32,4096]{1,0:T(8,128)(2,1)}), bf16[1024,4096]{1,0:T(8,128)(2,1)}) %all-gather.19.cloned.1.call-update) | async-done | bytes 8388624 | tf_op jit(solution)/shard_map/all_gather | solution.py:197
  427.5 7.7 fusion.19
  435.2 71.3 %all-gather.21.cloned.1.call-done = bf16[1024,4096]{1,0:T(8,128)(2,1)} async-done(((bf16[32,4096]{1,0:T(8,128)(2,1)}), bf16[1024,4096]{1,0:T(8,128)(2,1)}) %all-gather.21.cloned.1.call-update) | async-done | bytes 8388624 | tf_op jit(solution)/shard_map/all_gather | solution.py:198
  506.5 7.7 fusion.20
  514.2 71.3 %all-gather.23.cloned.1.call-done = bf16[4096,1024]{1,0:T(8,128)(2,1)} async-done(((bf16[128,1024]{1,0:T(8,128)(2,1)}), bf16[4096,1024]{1,0:T(8,128)(2,1)}) %all-gather.23.cloned.1.call-update) | async-done | bytes 8388624 | tf_op jit(solution)/shard_map/all_gather | solution.py:199
  585.6 12.9 multiply_convert_fusion.1
  598.5 7.3 fusion.21
  605.8 2.7 multiply_reduce_fusion.1
  612.2 2.5 broadcast.218.clone
  614.7 2.6 broadcast.218.clone2
  617.3 99.7 %while.39 = (s32[]{:T(128)}, bf16[2,128,1024]{2,1,0:T(8,128)(2,1)}, bf16[2,1024,1024]{2,1,0:T(8,128)(2,1)}, bf16[2,1024,1024]{2,1,0:T(8,128)(2,1)}, bf16[2,1024,...) while((s32[]{:T(128)}, bf16[2,128,1024]{2,1,0:T(8,128)(2,1)}, ...), condition=%wide.region_9.10_spmd.clone, body=%wide.region_7.9_spmd.clone.sunk | while | flops 341376512 | bytes 38882680 | solution.py:171
  718.1 2.8 convolution_bitcast_fusion.2
  721.0 2.7 fusion.12
  724.0 79.7 %reduce-scatter.10.cloned.1.call-done = bf16[2,128,1024]{2,1,0:T(8,128)(2,1)} async-done(((bf16[2,1024,1024]{2,1,0:T(8,128)(2,1)}), bf16[2,128,1024]{2,1,0:T(8,128)(2,1)}) %reduce-scatter.10.cloned.1.call-update) | async-done | bytes 524304 | tf_op jit(solution)/shard_map/reduce_scatter | solution.py:264
  803.8 3.8 convolution_bitcast_fusion.1
  807.7 87.7 %reduce-scatter.12.cloned.1.call-done = bf16[2,128,1024]{2,1,0:T(8,128)(2,1)} async-done(((bf16[2,1024,1024]{2,1,0:T(8,128)(2,1)}), bf16[2,128,1024]{2,1,0:T(8,128)(2,1)}) %reduce-scatter.12.cloned.1.call-update) | async-done | bytes 524304 | tf_op jit(solution)/shard_map/reduce_scatter | solution.py:267
  895.4 3.9 convolution_bitcast_fusion
  899.3 9.7 fusion.23
  909.1 9.7 fusion.24
  919.9 9.7 fusion.25
  932.1 7.3 fusion.11
  942.2 42.2 %all-reduce.4 = (f32[1024]{0:T(1024)S(1)}, f32[1024]{0:T(1024)S(1)}) all-reduce(f32[1024]{0:T(1024)S(1)} %get-tuple-element.554, f32[1024]{0:T(1024)S(1)} %get-tuple-element.552), channel_id=4, replica_groups=mesh['dp'=4,'ctx'=8] {'dp','ctx'}, use_global_device_ids=true, to_apply=%region_14.15.clone | all-reduce | flops 2048 | bytes 16384
  986.8 55.1 %reduce-scatter.14.cloned.1.call-done = f32[32,1024]{1,0:T(8,128)} async-done(((f32[1024,1024]{1,0:T(8,128)}), f32[32,1024]{1,0:T(8,128)}) %reduce-scatter.14.cloned.1.call-update) | async-done | bytes 131088 | tf_op jit(solution)/shard_map/reduce_scatter | solution.py:288
  1041.9 142.9 %reduce-scatter.20.cloned.1.call-done = f32[32,1024]{1,0:T(8,128)} async-done(((f32[1024,1024]{1,0:T(8,128)}), f32[32,1024]{1,0:T(8,128)}) %reduce-scatter.20.cloned.1.call-update) | async-done | bytes 131088 | tf_op jit(solution)/shard_map/reduce_scatter | solution.py:291
  1184.8 143.9 %reduce-scatter.16.cloned.1.call-done = f32[32,1024]{1,0:T(8,128)} async-done(((f32[1024,1024]{1,0:T(8,128)}), f32[32,1024]{1,0:T(8,128)}) %reduce-scatter.16.cloned.1.call-update) | async-done | bytes 131088 | tf_op jit(solution)/shard_map/reduce_scatter | solution.py:289
  1328.8 143.8 %reduce-scatter.18.cloned.1.call-done = f32[32,1024]{1,0:T(8,128)} async-done(((f32[1024,1024]{1,0:T(8,128)}), f32[32,1024]{1,0:T(8,128)}) %reduce-scatter.18.cloned.1.call-update) | async-done | bytes 131088 | tf_op jit(solution)/shard_map/reduce_scatter | solution.py:290
  1472.6 358.9 %reduce-scatter.22.cloned.1.call-done = f32[32,4096]{1,0:T(8,128)} async-done(((f32[1024,4096]{1,0:T(8,128)}), f32[32,4096]{1,0:T(8,128)}) %reduce-scatter.22.cloned.1.call-update) | async-done | bytes 524304 | tf_op jit(solution)/shard_map/reduce_scatter | solution.py:293
  1831.4 360.1 %reduce-scatter.24.cloned.1.call-done = f32[32,4096]{1,0:T(8,128)} async-done(((f32[1024,4096]{1,0:T(8,128)}), f32[32,4096]{1,0:T(8,128)}) %reduce-scatter.24.cloned.1.call-update) | async-done | bytes 524304 | tf_op jit(solution)/shard_map/reduce_scatter | solution.py:294
  2191.5 360.1 %reduce-scatter.26.cloned.1.call-done = f32[128,1024]{1,0:T(8,128)} async-done(((f32[4096,1024]{1,0:T(8,128)}), f32[128,1024]{1,0:T(8,128)}) %reduce-scatter.26.cloned.1.call-update) | async-done | bytes 524304 | tf_op jit(solution)/shard_map/reduce_scatter | solution.py:295
  (394 shorter events, 181.9 us)
Async XLA Ops:
  7.2 63.1 %all-gather.13.cloned.1.call-start = ((), (), s32[]{:S(2)}) async-start(), calls=%async_computation.11 | async-start | bytes 2162688 | tf_op jit(solution)/shard_map/all_gather | solution.py:193
  7.9 120.8 %all-gather.9.cloned.1.call-start = ((), (), s32[]{:S(2)}) async-start(), calls=%async_computation.9 | async-start | bytes 2162688 | tf_op jit(solution)/shard_map/all_gather | solution.py:194
  8.7 194.6 %all-gather.11.cloned.1.call-start = ((), (), s32[]{:S(2)}) async-start(), calls=%async_computation.10 | async-start | bytes 2162688 | tf_op jit(solution)/shard_map/all_gather | solution.py:192
  9.4 281.4 %all-gather.15.cloned.1.call-start = ((), (), s32[]{:S(2)}) async-start(), calls=%async_computation.12 | async-start | bytes 4718592 | tf_op jit(solution)/shard_map/all_gather | solution.py:217
  56.3 118.8 %copy-start.23 = (s32[2,1024]{1,0:T(2,128)S(1)}, s32[2,1024]{1,0:T(2,128)}, u32[]{:S(2)}) copy-start(s32[2,1024]{1,0:T(2,128)} %param.17) | copy-start | bytes 24580
  73.6 274.8 %all-gather.17.cloned.1.call-start = ((), (), s32[]{:S(2)}) async-start(), calls=%async_computation.13 | async-start | bytes 2162688 | tf_op jit(solution)/shard_map/all_gather | solution.py:195
  74.2 353.3 %all-gather.19.cloned.1.call-start = ((), (), s32[]{:S(2)}) async-start(), calls=%async_computation.14 | async-start | bytes 8650752 | tf_op jit(solution)/shard_map/all_gather | solution.py:197
  74.8 431.7 %all-gather.21.cloned.1.call-start = ((), (), s32[]{:S(2)}) async-start(), calls=%async_computation.15 | async-start | bytes 8650752 | tf_op jit(solution)/shard_map/all_gather | solution.py:198
  75.5 510.0 %all-gather.23.cloned.1.call-start = ((), (), s32[]{:S(2)}) async-start(), calls=%async_computation.16 | async-start | bytes 8650752 | tf_op jit(solution)/shard_map/all_gather | solution.py:199
  131.0 17.6 collective-permute-start
  148.6 23.9 collective-permute-start.1
  148.6 26.5 %collective-permute-start.4 = (bf16[2,128,1024]{2,1,0:T(8,128)(2,1)S(1)}, bf16[2,128,1024]{2,1,0:T(8,128)(2,1)S(1)}, u32[]{:S(2)}, u32[]{:S(2)}) collective-permute-start(bf16[2,128,1024]{2,1,0:T(8,128)(2,1)S(1)} %bitcast.192), channel_id=1, source_target_pairs={{1,0},{2,1},{3,2},{4,3},{5,4},{6,5},{7,6},{0,7},{9,8},{10,9},{11,1... | collective-permute-start | bytes 1572872 | tf_op jit(solution)/shard_map/ppermute | solution.py:30
  172.5 28.1 %collective-permute-start.2 = (bf16[2,128,1024]{2,1,0:T(8,128)(2,1)S(1)}, bf16[2,128,1024]{2,1,0:T(8,128)(2,1)S(1)}, u32[]{:S(2)}, u32[]{:S(2)}) collective-permute-start(bf16[2,128,1024]{2,1,0:T(8,128)(2,1)S(1)} %collective-permute-done.1), channel_id=1, source_target_pairs={{0,1},{1,2},{2,3},{3,4},{4,5},{5,6},{6,7},{7,0},{8,9},{9,10},{10,1... | collective-permute-start | bytes 1572872 | tf_op jit(solution)/shard_map/ppermute | solution.py:26
  175.0 628.7 %reduce-scatter.10.cloned.1.call-start = ((), (), s32[]{:S(2)}) async-start(), calls=%async_computation.17 | async-start | bytes 4718592 | tf_op jit(solution)/shard_map/reduce_scatter | solution.py:264
  175.2 33.2 %collective-permute-start.5 = (bf16[2,128,1024]{2,1,0:T(8,128)(2,1)S(1)}, bf16[2,128,1024]{2,1,0:T(8,128)(2,1)}, u32[]{:S(2)}, u32[]{:S(2)}) collective-permute-start(bf16[2,128,1024]{2,1,0:T(8,128)(2,1)S(1)} %collective-permute-done.4), channel_id=1, source_target_pairs={{1,0},{2,1},{3,2},{4,3},{5,4},{6,5},{7,6},{0,7},{9,8},{10,9},{11,1... | collective-permute-start | bytes 1572872 | tf_op jit(solution)/shard_map/ppermute | solution.py:30
  200.6 15.6 collective-permute-start.3
  208.4 24.5 collective-permute-start.6
  290.9 57.5 %copy-start.3 = (bf16[2,128,1024]{2,1,0:T(8,128)(2,1)S(1)}, bf16[2,128,1024]{2,1,0:T(8,128)(2,1)}, u32[]{:S(2)}) copy-start(bf16[2,128,1024]{2,1,0:T(8,128)(2,1)} %param.16) | copy-start | bytes 1572868
  328.3 106.9 %copy-start.13 = (bf16[2,128,1024]{2,1,0:T(8,128)(2,1)}, bf16[2,128,1024]{2,1,0:T(8,128)(2,1)S(1)}, u32[]{:S(2)}) copy-start(bf16[2,128,1024]{2,1,0:T(8,128)(2,1)S(1)} %get-tuple-element.432) | copy-start | bytes 1572868
  350.8 257.7 %copy-start.7 = (f32[256,1024]{1,0:T(8,128)}, f32[256,1024]{1,0:T(8,128)S(1)}, u32[]{:S(2)}) copy-start(f32[256,1024]{1,0:T(8,128)S(1)} %get-tuple-element.616) | copy-start | bytes 3145732
  351.0 155.6 %copy-start.10 = (bf16[256,1024]{1,0:T(8,128)(2,1)}, bf16[256,1024]{1,0:T(8,128)(2,1)S(1)}, u32[]{:S(2)}) copy-start(bf16[256,1024]{1,0:T(8,128)(2,1)S(1)} %multiply_convert_fusion.5) | copy-start | bytes 1572868
  435.2 150.3 %copy-start.19 = (bf16[2,128,1024]{2,1,0:T(8,128)(2,1)S(1)}, bf16[2,128,1024]{2,1,0:T(8,128)(2,1)}, u32[]{:S(2)}) copy-start(bf16[2,128,1024]{2,1,0:T(8,128)(2,1)} %param.27) | copy-start | bytes 1572868
  598.5 7.3 copy-start.22
  598.5 7.3 copy-start.21
  598.5 7.3 copy-start.26
  605.8 4.0 copy-start.9
  618.3 4.8 copy-start.1
  630.8 4.8 copy-start.1
  643.3 4.8 copy-start.1
  655.8 4.8 copy-start.1
  668.2 4.8 copy-start.1
  680.6 4.8 copy-start.1
  693.1 4.8 copy-start.1
  705.6 4.8 copy-start.1
  717.0 178.4 %reduce-scatter.12.cloned.1.call-start = ((), (), s32[]{:S(2)}) async-start(), calls=%async_computation.18 | async-start | bytes 4718592 | tf_op jit(solution)/shard_map/reduce_scatter | solution.py:267
  717.6 324.4 %reduce-scatter.14.cloned.1.call-start = ((), (), s32[]{:S(2)}) async-start(), calls=%async_computation.19 | async-start | bytes 4325376 | tf_op jit(solution)/shard_map/reduce_scatter | solution.py:288
  718.1 2.9 copy-start.6
  718.1 2.9 copy-start.14
  721.0 463.9 %reduce-scatter.20.cloned.1.call-start = ((), (), s32[]{:S(2)}) async-start(), calls=%async_computation.22 | async-start | bytes 4325376 | tf_op jit(solution)/shard_map/reduce_scatter | solution.py:291
  723.8 605.0 %reduce-scatter.16.cloned.1.call-start = ((), (), s32[]{:S(2)}) async-start(), calls=%async_computation.20 | async-start | bytes 4325376 | tf_op jit(solution)/shard_map/reduce_scatter | solution.py:289
  807.6 91.7 %copy-start.11 = (bf16[256,1024]{1,0:T(8,128)(2,1)S(1)}, bf16[256,1024]{1,0:T(8,128)(2,1)}, u32[]{:S(2)}) copy-start(bf16[256,1024]{1,0:T(8,128)(2,1)} %copy-done.10) | copy-start | bytes 1572868
  807.6 664.9 %reduce-scatter.18.cloned.1.call-start = ((), (), s32[]{:S(2)}) async-start(), calls=%async_computation.21 | async-start | bytes 4325376 | tf_op jit(solution)/shard_map/reduce_scatter | solution.py:290
  899.2 932.2 %reduce-scatter.22.cloned.1.call-start = ((), (), s32[]{:S(2)}) async-start(), calls=%async_computation.23 | async-start | bytes 17301504 | tf_op jit(solution)/shard_map/reduce_scatter | solution.py:293
  909.1 1282.4 %reduce-scatter.24.cloned.1.call-start = ((), (), s32[]{:S(2)}) async-start(), calls=%async_computation.24 | async-start | bytes 17301504 | tf_op jit(solution)/shard_map/reduce_scatter | solution.py:294
  918.8 1632.7 %reduce-scatter.26.cloned.1.call-start = ((), (), s32[]{:S(2)}) async-start(), calls=%async_computation.25 | async-start | bytes 17301504 | tf_op jit(solution)/shard_map/reduce_scatter | solution.py:295
  929.6 2.5 copy-start.8
  932.0 7.3 copy-start.15
  932.1 7.3 copy-start.17
  (24 other events, 31.7 us)
Sparse Core Ops, SparseCore 0:
  11.0 59.2 all-gather.12
  73.3 55.3 all-gather.8
  131.7 71.2 all-gather.10
  205.4 85.3 all-gather.14
  293.6 54.7 all-gather.16
  351.2 76.2 all-gather.18
  430.5 75.9 all-gather.20
  509.5 75.9 all-gather.22
  717.1 86.6 reduce-scatter.9
  807.7 87.6 reduce-scatter.11
  898.2 143.6 reduce-scatter.13
  1044.6 140.1 reduce-scatter.19
  1187.7 141.0 reduce-scatter.15
  1331.5 141.0 reduce-scatter.17
  1475.3 356.1 reduce-scatter.21
  1834.2 357.2 reduce-scatter.23
  2194.2 357.3 reduce-scatter.25
